TPU v7x, 512 devices: a whole 4x4x16 slice. The times are simulated.
512 devices in a mesh: tm: 8 (over y, core), space: 64 (over z, x).
Axes of the slice: x: 4, y: 4, z: 16, core: 2. Of those that a mesh axis runs over, the one named last changes fastest.
Arguments:
- snapshots: bfloat16 [128, 128, 16384], P('tm', None, 'space'), as said below
- frequencies: int32 [16], replicated, may hold values from 1 to 63, as said below
- offsets: int32 [128], P('tm'), may hold values from 0 to 16383
Outputs:
- modes: float32 [16, 2, 128, 16384], P('tm', None, None, 'space')
Inputs may be any that keep to these rules, and one draw needn't show every extreme that they name: `frequencies`: the kept frequency indices are distinct and include 1 and 63. `snapshots`: snapshot values of the record.
All inputs are finite; a program needn't handle non-finite values.
Results may differ from a plain program's by a relative error of at most 0.0041.
Values may be sent and summed in bfloat16 or wider, within the bound.
A program may use at most 64 MiB of HBM per device.

v0:
```python
import math

import jax
import jax.numpy as jnp
from jax import lax
from jax.sharding import PartitionSpec as P


def make_angle_table(frequencies, length):
    positions = jnp.arange(length, dtype=jnp.int32)
    turn_counts = frequencies[None, :] * positions[:, None] % length
    radians = turn_counts.astype(jnp.float32) * (2.0 * math.pi / length)
    window = 0.5 - 0.5 * jnp.cos(positions.astype(jnp.float32) * (2.0 * math.pi / length))
    cosine_cols = window[:, None] * jnp.cos(radians)
    sine_cols = window[:, None] * jnp.sin(radians)
    return jnp.concatenate([cosine_cols, sine_cols], axis=1).astype(jnp.bfloat16)


def embed_gram(gram_real, gram_imag):
    top_rows = jnp.stack([gram_real, -gram_imag], axis=-1)
    low_rows = jnp.stack([gram_imag, gram_real], axis=-1)
    order = gram_real.shape[0]
    return jnp.stack([top_rows, low_rows], axis=1).reshape(2 * order, 2 * order)


def local_gram(real_rows, imag_rows):
    real_gram = jnp.dot(real_rows, real_rows.T, preferred_element_type=jnp.float32) + jnp.dot(
        imag_rows, imag_rows.T, preferred_element_type=jnp.float32
    )
    cross = jnp.dot(imag_rows, real_rows.T, preferred_element_type=jnp.float32)
    imag_gram = cross - cross.T
    return jnp.stack([real_gram, imag_gram])


def unpack_gram(packed):
    return (packed[0], packed[1])


def finish_modes(packed, real_rows, imag_rows, total_cells):
    gram_real, gram_imag = unpack_gram(packed)
    embedded = embed_gram(gram_real / total_cells, gram_imag / total_cells)
    lower_factor = jnp.linalg.cholesky(embedded)
    order = real_rows.shape[0]
    cells_here = real_rows.shape[1]
    stacked_rows = (
        jnp.stack([real_rows, imag_rows], axis=1).reshape(2 * order, cells_here).astype(jnp.float32)
    )
    solved = lax.linalg.triangular_solve(lower_factor, stacked_rows, left_side=True, lower=True)
    return jnp.transpose(solved.reshape(order, 2, cells_here), (1, 0, 2))


def local(snapshots, frequencies, offsets):
    length = snapshots.shape[1]
    count_all = frequencies.shape[0]
    angle_table = make_angle_table(frequencies, length)
    projected = jnp.einsum(
        "btc,tk->kbc", snapshots, angle_table, preferred_element_type=jnp.float32
    )
    cos_part = projected[:count_all]
    sin_part = projected[count_all:]
    turn_counts = frequencies[:, None] * offsets[None, :] % length
    phase = turn_counts.astype(jnp.float32) * (2.0 * math.pi / length)
    cos_phase = jnp.cos(phase)[:, :, None]
    sin_phase = jnp.sin(phase)[:, :, None]
    real_part = cos_part * cos_phase - sin_part * sin_phase
    imag_part = -(sin_part * cos_phase + cos_part * sin_phase)
    stacked = jnp.stack([real_part, imag_part]).astype(jnp.bfloat16)
    regrouped = lax.all_to_all(stacked, "tm", split_axis=1, concat_axis=2, tiled=True)
    cells_here = regrouped.shape[3]
    total_cells = cells_here * lax.axis_size("space")
    per_freq = [
        (regrouped[0, slot_index], regrouped[1, slot_index])
        for slot_index in range(regrouped.shape[1])
    ]
    local_grams = jnp.stack([local_gram(real_rows, imag_rows) for real_rows, imag_rows in per_freq])
    summed = lax.psum(local_grams, "space")
    results = [
        finish_modes(
            summed[slot_index], per_freq[slot_index][0], per_freq[slot_index][1], total_cells
        )
        for slot_index in range(len(per_freq))
    ]
    return jnp.stack(results)


def solution(mesh):
    placed = (P("tm", None, "space"), P(), P("tm"))
    return jax.shard_map(
        local, mesh=mesh, in_specs=placed, out_specs=P("tm", None, None, "space"), check_vma=False
    )
```

profile of v0, /device:TPU:8, one launch (start us, length us, event | category | flops | bytes accessed | tf_op | source)
XLA Modules:
  0.0 465.1 jit_solution(17110627762532385624)
XLA Ops:
  6.6 0.9 multiply_convert_fusion.1
  7.5 0.8 fusion.59
  8.7 0.8 copy.34
  9.5 9.1 %all-to-all-start = ((bf16[2,16,16,256]{3,2,0,1:T(8,128)(2,1)}), bf16[2,16,16,256]{3,2,0,1:T(8,128)(2,1)S(1)}, u32[]{:S(2)}, u32[]{:S(2)}) async-start(bf16[2,16,16,256]{3,2,0,1:T(8,128)(2,1)} %copy.34), calls=%async_computation | async-start | bytes 524288 | tf_op jit(solution)/shard_map/all_to_all | solution.py:68
  18.7 6.1 %all-to-all-done = bf16[2,16,16,256]{3,2,0,1:T(8,128)(2,1)S(1)} async-done(((bf16[2,16,16,256]{3,2,0,1:T(8,128)(2,1)}), bf16[2,16,16,256]{3,2,0,1:T(8,128)(2,1)S(1)}, u32[]{:S(2)}, u32[]{:S(2)}) %all-to-all-start) | async-done | bytes 262176 | tf_op jit(solution)/shard_map/all_to_all | solution.py:68
  26.0 0.7 pad_maximum_fusion.2
  27.7 261.0 %all-reduce.3.cloned.1.call-done = f32[2,2,128,128]{3,2,1,0:T(8,128)} async-done(((f32[2,2,128,128]{3,2,1,0:T(8,128)}), f32[2,2,128,128]{3,2,1,0:T(8,128)}) %all-reduce.3.cloned.1.call-update) | async-done | bytes 262160 | tf_op jit(solution)/shard_map/psum | solution.py:76
  288.7 1.0 fusion.20
  289.6 0.9 fusion.61
  290.6 8.8 %copy.39 = f32[128,2,128,2]{3,2,1,0:T(8,128)} copy(f32[128,2,128,2]{2,0,3,1:T(8,128)S(1)} %pad_maximum_fusion.3) | data formatting | bytes 524288 | tf_op jit(solution)/shard_map/stack | solution.py:23
  299.4 12.7 %reshape.178 = f32[256,256]{1,0:T(8,128)S(1)} reshape(f32[128,2,128,2]{3,2,1,0:T(8,128)} %copy.39) | data formatting | bytes 524288 | tf_op jit(solution)/shard_map/reshape | solution.py:23
  312.3 11.7 %cholesky.130 = f32[128,128]{1,0:T(8,128)S(1)} custom-call(f32[128,128]{1,0:T(8,128)S(1)} %cholesky.194), custom_call_target="Cholesky" | custom-call | tf_op jit(solution)/shard_map/jit(cholesky)/cholesky | solution.py:42
  324.1 9.8 %custom-call.13 = f32[1,128,128]{1,2,0:T(8,128)S(1)} custom-call(f32[1,128,128]{2,1,0:T(8,128)S(1)} %get-tuple-element.58), custom_call_target="InvertDiagBlocksLowerTriangular" | custom-call | tf_op jit(solution)/shard_map/jit(cholesky)/cholesky | solution.py:42
  334.4 11.7 %cholesky.147 = f32[128,128]{1,0:T(8,128)S(1)} custom-call(f32[128,128]{1,0:T(8,128)S(1)} %convolution_subtract_fusion.3), custom_call_target="Cholesky" | custom-call | tf_op jit(solution)/shard_map/jit(cholesky)/cholesky | solution.py:42
  346.1 0.7 compare_reduce_fusion.2
  346.8 0.6 compare_reduce_fusion.3
  348.9 4.1 while.4
  349.6 1.4 bitcast_dynamic-update-slice_fusion.4
  351.6 1.4 bitcast_dynamic-update-slice_fusion.4
  353.0 19.9 %custom-call.14 = f32[2,128,128]{1,2,0:T(8,128)S(1)} custom-call(f32[2,128,128]{2,1,0:T(8,128)S(1)} %get-tuple-element.21), custom_call_target="InvertDiagBlocksLowerTriangular" | custom-call | tf_op jit(solution)/shard_map/triangular_solve/custom-call.0 | solution.py:48
  374.1 8.7 %copy.43 = f32[128,2,128,2]{3,2,1,0:T(8,128)} copy(f32[128,2,128,2]{2,0,3,1:T(8,128)S(1)} %pad_maximum_fusion.5) | data formatting | bytes 524288 | tf_op jit(solution)/shard_map/stack | solution.py:23
  382.8 12.7 %reshape.180 = f32[256,256]{1,0:T(8,128)S(1)} reshape(f32[128,2,128,2]{3,2,1,0:T(8,128)} %copy.43) | data formatting | bytes 524288 | tf_op jit(solution)/shard_map/reshape | solution.py:23
  395.7 11.7 %cholesky.164 = f32[128,128]{1,0:T(8,128)S(1)} custom-call(f32[128,128]{1,0:T(8,128)S(1)} %cholesky.197), custom_call_target="Cholesky" | custom-call | tf_op jit(solution)/shard_map/jit(cholesky)/cholesky | solution.py:42
  407.4 9.8 %custom-call.15 = f32[1,128,128]{1,2,0:T(8,128)S(1)} custom-call(f32[1,128,128]{2,1,0:T(8,128)S(1)} %get-tuple-element.64), custom_call_target="InvertDiagBlocksLowerTriangular" | custom-call | tf_op jit(solution)/shard_map/jit(cholesky)/cholesky | solution.py:42
  417.7 11.7 %cholesky.181 = f32[128,128]{1,0:T(8,128)S(1)} custom-call(f32[128,128]{1,0:T(8,128)S(1)} %convolution_subtract_fusion.2), custom_call_target="Cholesky" | custom-call | tf_op jit(solution)/shard_map/jit(cholesky)/cholesky | solution.py:42
  429.5 0.7 compare_reduce_fusion
  430.2 0.6 compare_reduce_fusion.1
  432.2 4.1 while.5
  432.9 1.4 bitcast_dynamic-update-slice_fusion.5
  434.9 1.4 bitcast_dynamic-update-slice_fusion.5
  436.4 19.9 %custom-call.16 = f32[2,128,128]{1,2,0:T(8,128)S(1)} custom-call(f32[2,128,128]{2,1,0:T(8,128)S(1)} %get-tuple-element.22), custom_call_target="InvertDiagBlocksLowerTriangular" | custom-call | tf_op jit(solution)/shard_map/triangular_solve/custom-call.0 | solution.py:48
  457.4 0.8 pad_maximum_fusion
  (72 shorter events, 8.8 us)
Async XLA Ops:
  6.5 1.7 copy-start
  9.5 15.3 %all-to-all-start = ((bf16[2,16,16,256]{3,2,0,1:T(8,128)(2,1)}), bf16[2,16,16,256]{3,2,0,1:T(8,128)(2,1)S(1)}, u32[]{:S(2)}, u32[]{:S(2)}) async-start(bf16[2,16,16,256]{3,2,0,1:T(8,128)(2,1)} %copy.34), calls=%async_computation | async-start | bytes 524288 | tf_op jit(solution)/shard_map/all_to_all | solution.py:68
  18.6 270.0 %all-reduce.3.cloned.1.call-start = ((), (), s32[]{:S(2)}) async-start(), calls=%async_computation.1 | async-start | bytes 524288 | tf_op jit(solution)/shard_map/psum | solution.py:76
Sparse Core Ops, SparseCore 0:
  26.9 261.7 all-reduce.2
where the time goes:
time: 466 us; the launch traced here: 465 us
  waiting for transfers between devices  267 us (57%)
  other arithmetic  115 us (25%)
  local copies, waits for them, and re-layouts  53.6 us (12%)
  between operations  16.5 us (4%)
  starting transfers between devices  9.15 us (2%)
    psum x1, waiting for transfers between devices, local(): summed = lax.psum(local_grams, 'space')  261 us
    another operation x14, other arithmetic, finish_modes(): lower_factor = jnp.linalg.cholesky(embedded)  69.3 us
    another operation x7, other arithmetic, finish_modes(): lax.linalg.triangular_solve(lower_factor, stacked_rows, left_side=True, l...  39.9 us
    reshape x4, local copies, waits for them, and re-layouts, embed_gram(): return jnp.stack([top_rows, low_rows], axis=1).reshape(2 * order, 2 * order)  25.6 us
    another operation x2, local copies, waits for them, and re-layouts, embed_gram(): return jnp.stack([top_rows, low_rows], axis=1).reshape(2 * order, 2 * order)  17.5 us
  transfers between devices with their start and end apart: 2, of which 2 were waited for; matrix products, arithmetic and copies ran while one was open for 0% of the time, Pallas kernels for 0%

commit v1 on v0

v1 whole, which is shorter than its diff:
```python
import functools
import math

import jax
import jax.numpy as jnp
from jax import lax
from jax.experimental import pallas as pl
from jax.experimental.pallas import tpu as pltpu
from jax.sharding import PartitionSpec as P

F32 = jnp.float32
BF16 = jnp.bfloat16

MESH = pl.DeviceIdType.MESH


def exchange_kernel(
    nt, nx, nz, snap_ref, table_ref, rot_ref, q_ref, g_ref,
    work, send, part, got_x, part_z, got_z, ring_z,
    a_send, a_recv, x_send, x_recv, z_send, z_recv, y_send, y_recv, w_send, w_recv, own_sem,
):
    nf_all = rot_ref.shape[0] // 2
    blocks, _, cells = snap_ref.shape
    nf = nf_all // nt
    nb = blocks * nt
    me = lax.axis_index("tm")
    spot = lax.axis_index("space")
    my_z = spot // nx
    my_x = spot % nx

    def tm_peer(d):
        return (lax.rem(me + d, nt), spot)

    def x_peer(d):
        return (me, my_z * nx + lax.rem(my_x + d, nx))

    def z_peer(d):
        return (me, lax.rem(my_z + d, nz) * nx + my_x)

    barrier = pltpu.get_barrier_semaphore()
    for d in range(1, nt):
        pl.semaphore_signal(barrier, inc=1, device_id=tm_peer(d), device_id_type=MESH)
    for d in range(1, nx):
        pl.semaphore_signal(barrier, inc=1, device_id=x_peer(d), device_id_type=MESH)
    for d in range(1, nz):
        pl.semaphore_signal(barrier, inc=1, device_id=z_peer(d), device_id_type=MESH)

    table = table_ref[...]
    for b in range(blocks):
        both = jnp.dot(table, snap_ref[b], preferred_element_type=F32)
        cos_part, sin_part = both[:nf_all], both[nf_all:]
        cos_phase = rot_ref[:nf_all, b:b + 1]
        sin_phase = rot_ref[nf_all:, b:b + 1]
        base = b * 2 * nf_all
        real = cos_part * cos_phase - sin_part * sin_phase
        imag = -(sin_part * cos_phase + cos_part * sin_phase)
        for h in range(cells // 128):
            work[h, base:base + nf_all, :] = real[:, h * 128:(h + 1) * 128]
            work[h, base + nf_all:base + 2 * nf_all, :] = imag[:, h * 128:(h + 1) * 128]
    for j in range(nf_all):
        for half in range(2):
            for h in range(cells // 128):
                rows = work[h, pl.ds(half * nf_all + j, blocks, stride=2 * nf_all), :]
                send[j // nf, j % nf, half, :, h * 128:(h + 1) * 128] = rows.astype(BF16)

    pl.semaphore_wait(barrier, nt - 1 + nx - 1 + nz - 1)

    def a_copy(d):
        return pltpu.make_async_remote_copy(
            src_ref=send.at[lax.rem(me + d, nt)],
            dst_ref=q_ref.at[:, :, pl.ds(pl.multiple_of(me * blocks, blocks), blocks), :],
            send_sem=a_send.at[d], recv_sem=a_recv.at[d],
            device_id=tm_peer(d), device_id_type=MESH)

    own = pltpu.make_async_copy(
        send.at[me], q_ref.at[:, :, pl.ds(pl.multiple_of(me * blocks, blocks), blocks), :], own_sem)
    for d in range(1, nt):
        a_copy(d).start()
    own.start()
    own.wait()
    for d in range(1, nt):
        a_copy(d).wait_recv()

    row = lax.broadcasted_iota(jnp.int32, (nb, nb), 0)
    lane = lax.broadcasted_iota(jnp.int32, (nb, nb), 1)
    for f in range(nf):
        rows = q_ref[f].reshape(2 * nb, cells)
        full = lax.dot_general(rows, rows, (((1,), (1,)), ((), ())), preferred_element_type=F32)
        real = full[:nb, :nb] + full[nb:, nb:]
        imag = full[nb:, :nb] - full[:nb, nb:]
        part[f * nb:(f + 1) * nb, :] = jnp.where(row >= lane, real, imag)

    wide = nf * nb // nx
    thin = wide // nz

    def x_copy(d):
        return pltpu.make_async_remote_copy(
            src_ref=part.at[pl.ds(pl.multiple_of(lax.rem(my_x + d, nx) * wide, wide), wide), :],
            dst_ref=got_x.at[d],
            send_sem=x_send.at[d], recv_sem=x_recv.at[d],
            device_id=x_peer(d), device_id_type=MESH)

    for d in range(1, nx):
        x_copy(d).start()
    total = part[pl.ds(pl.multiple_of(my_x * wide, wide), wide), :]
    for d in range(1, nx):
        x_copy(d).wait_recv()
        total = total + got_x[d]
    for c in range(nz):
        part_z[c] = total[c * thin:(c + 1) * thin, :]

    def z_copy(d):
        return pltpu.make_async_remote_copy(
            src_ref=part_z.at[lax.rem(my_z + d, nz)],
            dst_ref=got_z.at[d],
            send_sem=z_send.at[d], recv_sem=z_recv.at[d],
            device_id=z_peer(d), device_id_type=MESH)

    for d in range(1, nz):
        z_copy(d).start()
    small = part_z[my_z]
    for d in range(1, nz):
        z_copy(d).wait_recv()
        small = small + got_z[d]
    ring_z[my_z] = small

    def y_copy(d):
        return pltpu.make_async_remote_copy(
            src_ref=ring_z.at[my_z],
            dst_ref=ring_z.at[my_z],
            send_sem=y_send.at[d], recv_sem=y_recv.at[d],
            device_id=z_peer(d), device_id_type=MESH)

    for d in range(1, nz):
        y_copy(d).start()
    for d in range(1, nz):
        y_copy(d).wait_recv()
    for c in range(nz):
        got_x[0, c * thin:(c + 1) * thin, :] = ring_z[c]
    mine = pl.ds(pl.multiple_of(my_x * wide, wide), wide)
    g_ref[mine, :] = got_x[0]

    def w_copy(d):
        return pltpu.make_async_remote_copy(
            src_ref=got_x.at[0],
            dst_ref=g_ref.at[mine, :],
            send_sem=w_send.at[d], recv_sem=w_recv.at[d],
            device_id=x_peer(d), device_id_type=MESH)

    for d in range(1, nx):
        w_copy(d).start()
    for d in range(1, nx):
        w_copy(d).wait_recv()
    for d in range(1, nt):
        a_copy(d).wait_send()
    for d in range(1, nx):
        x_copy(d).wait_send()
        w_copy(d).wait_send()
    for d in range(1, nz):
        z_copy(d).wait_send()
        y_copy(d).wait_send()


def exchange(snapshots, table, rotation):
    nt = lax.axis_size("tm")
    nx = 4
    nz = lax.axis_size("space") // nx
    blocks, _, cells = snapshots.shape
    nf_all = rotation.shape[0] // 2
    nf, nb = nf_all // nt, blocks * nt
    wide = nf * nb // nx
    thin = wide // nz
    vm = pl.BlockSpec(memory_space=pltpu.VMEM)
    dma = pltpu.SemaphoreType.DMA
    q, g = pl.pallas_call(
        functools.partial(exchange_kernel, nt, nx, nz),
        out_shape=(jax.ShapeDtypeStruct((nf, 2, nb, cells), BF16), jax.ShapeDtypeStruct((nf * nb, nb), F32)),
        in_specs=[vm, vm, vm], out_specs=(vm, vm),
        scratch_shapes=[
            pltpu.VMEM((cells // 128, blocks * 2 * nf_all, 128), F32),
            pltpu.VMEM((nt, nf, 2, blocks, cells), BF16),
            pltpu.VMEM((nf * nb, nb), F32),
            pltpu.VMEM((nx, wide, nb), F32),
            pltpu.VMEM((nz, thin, nb), F32),
            pltpu.VMEM((nz, thin, nb), F32),
            pltpu.VMEM((nz, thin, nb), F32),
            dma((nt,)), dma((nt,)), dma((nx,)), dma((nx,)), dma((nz,)), dma((nz,)),
            dma((nz,)), dma((nz,)), dma((nx,)), dma((nx,)), dma,
        ],
        compiler_params=pltpu.CompilerParams(
            collective_id=0, has_side_effects=True, vmem_limit_bytes=24 << 20),
        name="exchange_gram",
    )(snapshots, table, rotation)
    return q, g.reshape(nf, nb, nb)


def split2(v):
    hi = v.astype(BF16)
    lo = (v - hi.astype(F32)).astype(BF16)
    return hi, lo


def lane_bcast(v, col):
    return jnp.broadcast_to(v[:, col:col + 1], v.shape)


def factor_kernel(scale, block, q_ref, g_ref, out_ref, m_re, m_im, w_ref):
    nf, _, nb, cells = q_ref.shape
    row8 = lax.broadcasted_iota(jnp.int32, (8, nb), 0)
    lane8 = lax.broadcasted_iota(jnp.int32, (8, nb), 1)
    row = lax.broadcasted_iota(jnp.int32, (nb, nb), 0)
    lane = lax.broadcasted_iota(jnp.int32, (nb, nb), 1)
    for f in range(nf):
        packed = g_ref[f] * scale
        flipped = packed.T
        m_re[f] = jnp.where(row >= lane, packed, flipped)
        m_im[f] = jnp.where(row > lane, -flipped, jnp.where(row < lane, packed, 0.0))
    per = block // 8
    for k in range(nb // block):
        r0 = k * block
        R = [
            [[m_re[f, r0 + 8 * v:r0 + 8 * v + 8, :] for v in range(per)],
             [m_im[f, r0 + 8 * v:r0 + 8 * v + 8, :] for v in range(per)]]
            for f in range(nf)
        ]
        dsel = [[jnp.ones((8, nb), F32) for v in range(per)] for f in range(nf)]
        for p in range(block):
            v0, s = p // 8, p % 8
            col = r0 + p
            at_col = lane8 == col
            for f in range(nf):
                re, im = R[f]
                p_re = jnp.broadcast_to(re[v0][s:s + 1, :], (8, nb))
                p_im = jnp.broadcast_to(im[v0][s:s + 1, :], (8, nb))
                d = lane_bcast(p_re, col)
                inv = 1.0 / d
                dsel[f][v0] = jnp.where(row8 == s, d, dsel[f][v0])
                u_re = jnp.where(at_col, inv, p_re * inv)
                u_im = jnp.where(at_col, 0.0, p_im * inv)
                for v in range(v0, per):
                    if v == v0 and s == 7:
                        continue
                    c_re = lane_bcast(re[v], col)
                    c_im = lane_bcast(im[v], col)
                    if v == v0:
                        below = row8 > s
                        c_re = jnp.where(below, c_re, 0.0)
                        c_im = jnp.where(below, c_im, 0.0)
                        zap = at_col & below
                    else:
                        zap = at_col
                    b_re = jnp.where(zap, 0.0, re[v])
                    b_im = jnp.where(zap, 0.0, im[v])
                    re[v] = b_re - (c_re * u_re - c_im * u_im)
                    im[v] = b_im - (c_re * u_im + c_im * u_re)
        for f in range(nf):
            re, im = R[f]
            n_re, n_im = [], []
            for v in range(per):
                mine = row8 + (r0 + 8 * v)
                rs = lax.rsqrt(dsel[f][v])
                cut = (lane8 > mine) & (lane8 < r0 + block)
                n_re.append(jnp.where(cut, 0.0, jnp.where(lane8 == mine, rs, re[v] * rs)))
                n_im.append(jnp.where(cut | (lane8 == mine), 0.0, im[v] * rs))
            a_re = jnp.concatenate(n_re, axis=0)
            a_im = jnp.concatenate(n_im, axis=0)
            keep = lax.broadcasted_iota(jnp.int32, (block, nb), 1) < r0 + block
            w_ref[f, 0, r0:r0 + block, :] = jnp.where(keep, a_re, 0.0)
            w_ref[f, 1, r0:r0 + block, :] = jnp.where(keep, a_im, 0.0)
            if k + 1 < nb // block:
                rest = nb - r0 - block
                left = jnp.concatenate([a_re, a_im], axis=0).T[r0 + block:, :]
                right = jnp.concatenate(
                    [jnp.concatenate([a_re, a_im], axis=1), jnp.concatenate([a_im, -a_re], axis=1)], axis=0)
                lh, ll = split2(left)
                rh, rl = split2(right)
                lcat = jnp.concatenate([lh, lh, ll], axis=1)
                rcat = jnp.concatenate([rh, rl, rh], axis=0)
                upd = jnp.dot(lcat, rcat, preferred_element_type=F32)
                inside = lax.broadcasted_iota(jnp.int32, (rest, nb), 1)
                inside = (inside >= r0) & (inside < r0 + block)
                m_re[f, r0 + block:, :] = jnp.where(inside, 0.0, m_re[f, r0 + block:, :]) - upd[:, :nb]
                m_im[f, r0 + block:, :] = jnp.where(inside, 0.0, m_im[f, r0 + block:, :]) - upd[:, nb:]
    for f in range(nf):
        w_re, w_im = w_ref[f, 0], w_ref[f, 1]
        rh, rl = split2(w_re)
        ih, il = split2(w_im)
        x_re, x_im = q_ref[f, 0], q_ref[f, 1]
        x = jnp.concatenate([x_re, x_im], axis=0)
        a = jnp.concatenate([rh, -ih], axis=1)
        al = jnp.concatenate([rl, -il], axis=1)
        b = jnp.concatenate([ih, rh], axis=1)
        bl = jnp.concatenate([il, rl], axis=1)
        out_ref[f, 0] = jnp.dot(a, x, preferred_element_type=F32) + jnp.dot(al, x, preferred_element_type=F32)
        out_ref[f, 1] = jnp.dot(b, x, preferred_element_type=F32) + jnp.dot(bl, x, preferred_element_type=F32)


def finish(q, g, scale, block=32):
    nf, _, nb, cells = q.shape
    vm = pl.BlockSpec(memory_space=pltpu.VMEM)
    return pl.pallas_call(
        functools.partial(factor_kernel, scale, block),
        out_shape=jax.ShapeDtypeStruct((nf, 2, nb, cells), F32),
        in_specs=[vm, vm], out_specs=vm,
        scratch_shapes=[pltpu.VMEM((nf, nb, nb), F32), pltpu.VMEM((nf, nb, nb), F32), pltpu.VMEM((nf, 2, nb, nb), F32)],
        compiler_params=pltpu.CompilerParams(vmem_limit_bytes=32 << 20),
        name="factor_apply",
    )(q, g)


def make_angle_table(frequencies, length):
    positions = jnp.arange(length, dtype=jnp.int32)
    turn_counts = frequencies[:, None] * positions[None, :] % length
    radians = turn_counts.astype(jnp.float32) * (2.0 * math.pi / length)
    window = 0.5 - 0.5 * jnp.cos(positions.astype(jnp.float32) * (2.0 * math.pi / length))
    cosine_rows = window[None, :] * jnp.cos(radians)
    sine_rows = window[None, :] * jnp.sin(radians)
    return jnp.concatenate([cosine_rows, sine_rows], axis=0).astype(jnp.bfloat16)


def local(snapshots, frequencies, offsets):
    length = snapshots.shape[1]
    table = make_angle_table(frequencies, length)
    turn_counts = frequencies[:, None] * offsets[None, :] % length
    phase = turn_counts.astype(jnp.float32) * (2.0 * math.pi / length)
    rotation = jnp.concatenate([jnp.cos(phase), jnp.sin(phase)], axis=0)
    total_cells = snapshots.shape[2] * lax.axis_size("space")
    q, g = exchange(snapshots, table, rotation)
    return finish(q, g, 1.0 / total_cells)


def solution(mesh):
    placed = (P("tm", None, "space"), P(), P("tm"))
    return jax.shard_map(
        local, mesh=mesh, in_specs=placed, out_specs=P("tm", None, None, "space"), check_vma=False
    )
```

time: 466 us -> 66.8 us (0.14)
  the two profiles are of different devices: /device:TPU:8 before, /device:TPU:4 now
where the time goes in v1:
time: 66.8 us; the launch traced here: 66.6 us
  Pallas kernels  63.8 us (96%)
  local copies, waits for them, and re-layouts  2.47 us (4%)
    pallas_call x1, Pallas kernels, exchange(): pl.pallas_call(functools.partial(exchange_kernel, nt, nx, nz), out_shape=...  45.4 us
    pallas_call x1, Pallas kernels, finish(): pl.pallas_call(functools.partial(factor_kernel, scale, block), out_shape=...  18.4 us
    unnamed x6, local copies, waits for them, and re-layouts  2.47 us

profile of v1, /device:TPU:4, one launch (start us, length us, event | category | flops | bytes accessed | tf_op | source)
XLA Modules:
  0.0 66.6 jit_solution(18387252693569851007)
XLA Ops:
  0.0 0.0 copy-start.1
  0.0 0.6 copy-done.1
  0.7 0.1 multiply_convert_fusion.1
  0.8 0.0 copy-start.2
  0.8 0.6 copy-done.2
  1.4 0.1 fusion.10
  1.6 0.0 copy-start
  1.6 1.2 %copy-done = bf16[16,128,256]{2,1,0:T(8,128)(2,1)S(1)} copy-done((bf16[16,128,256]{2,1,0:T(8,128)(2,1)S(1)}, bf16[16,128,256]{2,1,0:T(8,128)(2,1)}, u32[]{:S(2)}) %copy-start) | copy-done | bytes 1048600
  2.8 45.4 %exchange_gram.1 = (bf16[2,2,128,256]{3,2,1,0:T(8,128)(2,1)S(1)}, f32[256,128]{1,0:T(8,128)S(1)}) custom-call(bf16[16,128,256]{2,1,0:T(8,128)(2,1)S(1)} %copy-done, bf16[32,128]{1,0:T(8,128)(2,1)S(1)} %pad_maximum_fusion.1.table_ref, f32[32,16]{1,0:T(8,128)S(1)} %pad_maximum_fusion.rot_ref), custom_call_target="tpu_custom_call" | custom-call | tf_op jit(solution)/shard_map/exchange_gram/pallas_call | solution.py:175
  48.2 18.4 %factor_apply.1 = f32[2,2,128,256]{3,2,1,0:T(8,128)} custom-call(bf16[2,2,128,256]{3,2,1,0:T(8,128)(2,1)S(1)} %get-tuple-element.7.q_ref, f32[2,128,128]{2,1,0:T(8,128)S(1)} %bitcast.1), custom_call_target="tpu_custom_call" | custom-call | tf_op jit(solution)/shard_map/factor_apply/pallas_call | solution.py:301
  (3 shorter events, 0.1 us)
Async XLA Ops:
  0.0 0.7 copy-start.1
  0.8 0.7 copy-start.2
  1.6 1.2 %copy-start = (bf16[16,128,256]{2,1,0:T(8,128)(2,1)S(1)}, bf16[16,128,256]{2,1,0:T(8,128)(2,1)}, u32[]{:S(2)}) copy-start(bf16[16,128,256]{2,1,0:T(8,128)(2,1)} %snap_ref.1) | copy-start | bytes 3145732

commit v2 on v1

v2 whole, which is shorter than its diff:
```python
import functools
import math

import jax
import jax.numpy as jnp
from jax import lax
from jax.experimental import pallas as pl
from jax.experimental.pallas import tpu as pltpu
from jax.sharding import PartitionSpec as P

F32 = jnp.float32
BF16 = jnp.bfloat16

MESH = pl.DeviceIdType.MESH
LANES = 128


def cos_sin(turns, length):
    quarter = length // 4
    shifted = turns + quarter // 2
    quadrant = lax.rem(lax.div(shifted, quarter), 4)
    theta = (lax.rem(shifted, quarter) - quarter // 2).astype(F32) * (2.0 * math.pi / length)
    sq = theta * theta
    cos_small = 1.0 + sq * (-0.5 + sq * (1 / 24 + sq * (-1 / 720 + sq * (1 / 40320 - sq / 3628800))))
    sin_small = theta * (1.0 + sq * (-1 / 6 + sq * (1 / 120 + sq * (-1 / 5040 + sq / 362880))))
    swap = (quadrant == 1) | (quadrant == 3)
    cos_sign = jnp.where((quadrant == 1) | (quadrant == 2), -1.0, 1.0)
    sin_sign = jnp.where(quadrant >= 2, -1.0, 1.0)
    return (
        jnp.where(swap, sin_small, cos_small) * cos_sign,
        jnp.where(swap, cos_small, sin_small) * sin_sign,
    )


def exchange_kernel(
    nt, nx, nl, nh, freq_ref, off_ref, snap_hbm, q_ref, g_ref,
    snap, work, send, part, got, half_sum, got_far,
    in_sem, a_send, a_recv, r_send, r_recv, f_send, f_recv, w_send, w_recv, own_sem,
):
    nf_all = freq_ref.shape[0]
    blocks, length, cells = snap.shape
    nf = nf_all // nt
    nb = blocks * nt
    halves = cells // LANES
    group = nx * nl
    me = lax.axis_index("tm")
    spot = lax.axis_index("space")
    my_far = lax.div(spot, group)
    my_near = lax.rem(spot, group)
    my_l = lax.div(my_near, nx)
    my_x = lax.rem(my_near, nx)

    def tm_peer(d):
        return (lax.rem(me + d, nt), spot)

    def near_slot(dl, dx):
        return lax.rem(my_l + dl, nl) * nx + lax.rem(my_x + dx, nx)

    def near_peer(dl, dx):
        return (me, my_far * group + near_slot(dl, dx))

    def far_peer(d):
        return (me, lax.rem(my_far + d, nh) * group + my_near)

    near = [(dl, dx) for dl in range(nl) for dx in range(nx) if dl or dx]

    barrier = pltpu.get_barrier_semaphore()
    for d in range(1, nh):
        pl.semaphore_signal(barrier, inc=1, device_id=far_peer(d), device_id_type=MESH)
    for d in range(1, nt):
        pl.semaphore_signal(barrier, inc=1, device_id=tm_peer(d), device_id_type=MESH)
    for dl, dx in near:
        pl.semaphore_signal(barrier, inc=1, device_id=near_peer(dl, dx), device_id_type=MESH)

    step = blocks // 4
    loads = [
        pltpu.make_async_copy(snap_hbm.at[pl.ds(i * step, step)], snap.at[pl.ds(i * step, step)], in_sem.at[i])
        for i in range(4)
    ]
    for load in loads:
        load.start()

    row = lax.broadcasted_iota(jnp.int32, (nf_all, length), 0)
    position = lax.broadcasted_iota(jnp.int32, (nf_all, length), 1)
    freq = jnp.zeros((nf_all, length), jnp.int32)
    start = jnp.zeros((nf_all, length), jnp.int32)
    for j in range(nf_all):
        freq = jnp.where(row == j, freq_ref[j], freq)
    for b in range(blocks):
        start = jnp.where(position == b, off_ref[b], start)
    window = 0.5 - 0.5 * cos_sin(position, length)[0]
    cosine, sine = cos_sin(lax.rem(freq * position, length), length)
    table = jnp.concatenate([window * cosine, window * sine], axis=0).astype(BF16)
    cos_phase, sin_phase = cos_sin(lax.rem(freq * lax.rem(start, length), length), length)

    for b in range(blocks):
        if b % step == 0:
            loads[b // step].wait()
        both = jnp.dot(table, snap[b], preferred_element_type=F32)
        cos_part, sin_part = both[:nf_all], both[nf_all:]
        cp, sp = cos_phase[:, b:b + 1], sin_phase[:, b:b + 1]
        base = b * 2 * nf_all
        real = cos_part * cp - sin_part * sp
        imag = -(sin_part * cp + cos_part * sp)
        for h in range(halves):
            work[h, base:base + nf_all, :] = real[:, h * LANES:(h + 1) * LANES]
            work[h, base + nf_all:base + 2 * nf_all, :] = imag[:, h * LANES:(h + 1) * LANES]

    mine = pl.ds(pl.multiple_of(me * blocks, blocks), blocks)

    def a_copy(h, d):
        return pltpu.make_async_remote_copy(
            src_ref=send.at[h, lax.rem(me + d, nt)],
            dst_ref=q_ref.at[:, :, mine, pl.ds(h * LANES, LANES)],
            send_sem=a_send.at[h, d], recv_sem=a_recv.at[h, d],
            device_id=tm_peer(d), device_id_type=MESH)

    own = [
        pltpu.make_async_copy(send.at[h, me], q_ref.at[:, :, mine, pl.ds(h * LANES, LANES)], own_sem.at[h])
        for h in range(halves)
    ]
    for h in range(halves):
        for j in range(nf_all):
            for ri in range(2):
                rows = work[h, pl.ds(ri * nf_all + j, blocks, stride=2 * nf_all), :]
                send[h, j // nf, j % nf, ri] = rows.astype(BF16)
        if h == 0:
            pl.semaphore_wait(barrier, nh - 1 + nt - 1 + group - 1)
        for d in range(1, nt):
            a_copy(h, d).start()
        own[h].start()
    for h in range(halves):
        own[h].wait()
        for d in range(1, nt):
            a_copy(h, d).wait_recv()

    grow = lax.broadcasted_iota(jnp.int32, (nb, nb), 0)
    glane = lax.broadcasted_iota(jnp.int32, (nb, nb), 1)
    for f in range(nf):
        rows = q_ref[f].reshape(2 * nb, cells)
        full = lax.dot_general(rows, rows, (((1,), (1,)), ((), ())), preferred_element_type=F32)
        real = full[:nb, :nb] + full[nb:, nb:]
        imag = full[nb:, :nb] - full[:nb, nb:]
        part[f * nb:(f + 1) * nb, :] = jnp.where(grow >= glane, real, imag)

    wide = nf * nb // group

    def chunk(slot):
        return pl.ds(pl.multiple_of(slot * wide, wide), wide)

    def r_copy(dl, dx):
        i = dl * nx + dx
        return pltpu.make_async_remote_copy(
            src_ref=part.at[chunk(near_slot(dl, dx)), :], dst_ref=got.at[i],
            send_sem=r_send.at[i], recv_sem=r_recv.at[i],
            device_id=near_peer(dl, dx), device_id_type=MESH)

    for dl, dx in near:
        r_copy(dl, dx).start()
    total = part[chunk(my_near), :]
    for dl, dx in near:
        r_copy(dl, dx).wait_recv()
        total = total + got[dl * nx + dx]
    got_far[my_far] = total
    half_sum[...] = total

    def f_copy(d):
        return pltpu.make_async_remote_copy(
            src_ref=half_sum, dst_ref=got_far.at[my_far],
            send_sem=f_send.at[d], recv_sem=f_recv.at[d],
            device_id=far_peer(d), device_id_type=MESH)

    for d in range(1, nh):
        f_copy(d).start()
    for d in range(1, nh):
        f_copy(d).wait_recv()
    total = got_far[0]
    for i in range(1, nh):
        total = total + got_far[i]
    g_ref[chunk(my_near), :] = total

    def w_copy(dl, dx):
        i = dl * nx + dx
        return pltpu.make_async_remote_copy(
            src_ref=g_ref.at[chunk(my_near), :], dst_ref=g_ref.at[chunk(my_near), :],
            send_sem=w_send.at[i], recv_sem=w_recv.at[i],
            device_id=near_peer(dl, dx), device_id_type=MESH)

    for dl, dx in near:
        w_copy(dl, dx).start()
    for h in range(halves):
        for d in range(1, nt):
            a_copy(h, d).wait_send()
    for dl, dx in near:
        r_copy(dl, dx).wait_send()
    for d in range(1, nh):
        f_copy(d).wait_send()
    for dl, dx in near:
        w_copy(dl, dx).wait_recv()
    for dl, dx in near:
        w_copy(dl, dx).wait_send()


def exchange(snapshots, frequencies, offsets):
    nt = lax.axis_size("tm")
    nx, nl = 4, 4
    group = nx * nl
    nh = lax.axis_size("space") // group
    blocks, length, cells = snapshots.shape
    nf_all = frequencies.shape[0]
    nf, nb = nf_all // nt, blocks * nt
    wide = nf * nb // group
    halves = cells // LANES
    vm = pl.BlockSpec(memory_space=pltpu.VMEM)
    sm = pl.BlockSpec(memory_space=pltpu.SMEM)
    dma = pltpu.SemaphoreType.DMA
    q, g = pl.pallas_call(
        functools.partial(exchange_kernel, nt, nx, nl, nh),
        out_shape=(jax.ShapeDtypeStruct((nf, 2, nb, cells), BF16), jax.ShapeDtypeStruct((nf * nb, nb), F32)),
        in_specs=[sm, sm, pl.BlockSpec(memory_space=pltpu.HBM)], out_specs=(vm, vm),
        scratch_shapes=[
            pltpu.VMEM((blocks, length, cells), BF16),
            pltpu.VMEM((halves, blocks * 2 * nf_all, LANES), F32),
            pltpu.VMEM((halves, nt, nf, 2, blocks, LANES), BF16),
            pltpu.VMEM((nf * nb, nb), F32),
            pltpu.VMEM((group, wide, nb), F32),
            pltpu.VMEM((wide, nb), F32),
            pltpu.VMEM((nh, wide, nb), F32),
            dma((4,)), dma((halves, nt)), dma((halves, nt)), dma((group,)), dma((group,)),
            dma((nh,)), dma((nh,)), dma((group,)), dma((group,)), dma((halves,)),
        ],
        compiler_params=pltpu.CompilerParams(
            collective_id=0, has_side_effects=True, vmem_limit_bytes=63 << 20),
        name="exchange_gram",
    )(frequencies, offsets, snapshots)
    return q, g.reshape(nf, nb, nb)


def split2(v):
    hi = v.astype(BF16)
    lo = (v - hi.astype(F32)).astype(BF16)
    return hi, lo


def lane_bcast(v, col):
    return jnp.broadcast_to(v[:, col:col + 1], v.shape)


def factor_kernel(scale, block, q_ref, g_ref, out_ref, m_re, m_im, w_ref):
    nf, _, nb, cells = q_ref.shape
    row8 = lax.broadcasted_iota(jnp.int32, (8, nb), 0)
    lane8 = lax.broadcasted_iota(jnp.int32, (8, nb), 1)
    row = lax.broadcasted_iota(jnp.int32, (nb, nb), 0)
    lane = lax.broadcasted_iota(jnp.int32, (nb, nb), 1)
    for f in range(nf):
        packed = g_ref[f] * scale
        flipped = packed.T
        m_re[f] = jnp.where(row >= lane, packed, flipped)
        m_im[f] = jnp.where(row > lane, -flipped, jnp.where(row < lane, packed, 0.0))
    per = block // 8
    for k in range(nb // block):
        r0 = k * block
        R = [
            [[m_re[f, r0 + 8 * v:r0 + 8 * v + 8, :] for v in range(per)],
             [m_im[f, r0 + 8 * v:r0 + 8 * v + 8, :] for v in range(per)]]
            for f in range(nf)
        ]
        dsel = [[jnp.ones((8, nb), F32) for v in range(per)] for f in range(nf)]
        for p in range(block):
            v0, s = p // 8, p % 8
            col = r0 + p
            at_col = lane8 == col
            for f in range(nf):
                re, im = R[f]
                p_re = jnp.broadcast_to(re[v0][s:s + 1, :], (8, nb))
                p_im = jnp.broadcast_to(im[v0][s:s + 1, :], (8, nb))
                d = lane_bcast(p_re, col)
                inv = 1.0 / d
                dsel[f][v0] = jnp.where(row8 == s, d, dsel[f][v0])
                u_re = jnp.where(at_col, inv, p_re * inv)
                u_im = jnp.where(at_col, 0.0, p_im * inv)
                for v in range(v0, per):
                    if v == v0 and s == 7:
                        continue
                    c_re = lane_bcast(re[v], col)
                    c_im = lane_bcast(im[v], col)
                    if v == v0:
                        below = row8 > s
                        c_re = jnp.where(below, c_re, 0.0)
                        c_im = jnp.where(below, c_im, 0.0)
                        zap = at_col & below
                    else:
                        zap = at_col
                    b_re = jnp.where(zap, 0.0, re[v])
                    b_im = jnp.where(zap, 0.0, im[v])
                    re[v] = b_re - (c_re * u_re - c_im * u_im)
                    im[v] = b_im - (c_re * u_im + c_im * u_re)
        for f in range(nf):
            re, im = R[f]
            n_re, n_im = [], []
            for v in range(per):
                mine = row8 + (r0 + 8 * v)
                rs = lax.rsqrt(dsel[f][v])
                cut = (lane8 > mine) & (lane8 < r0 + block)
                n_re.append(jnp.where(cut, 0.0, jnp.where(lane8 == mine, rs, re[v] * rs)))
                n_im.append(jnp.where(cut | (lane8 == mine), 0.0, im[v] * rs))
            a_re = jnp.concatenate(n_re, axis=0)
            a_im = jnp.concatenate(n_im, axis=0)
            keep = lax.broadcasted_iota(jnp.int32, (block, nb), 1) < r0 + block
            w_ref[f, 0, r0:r0 + block, :] = jnp.where(keep, a_re, 0.0)
            w_ref[f, 1, r0:r0 + block, :] = jnp.where(keep, a_im, 0.0)
            if k + 1 < nb // block:
                rest = nb - r0 - block
                left = jnp.concatenate([a_re, a_im], axis=0).T[r0 + block:, :]
                right = jnp.concatenate(
                    [jnp.concatenate([a_re, a_im], axis=1), jnp.concatenate([a_im, -a_re], axis=1)], axis=0)
                lh, ll = split2(left)
                rh, rl = split2(right)
                lcat = jnp.concatenate([lh, lh, ll], axis=1)
                rcat = jnp.concatenate([rh, rl, rh], axis=0)
                upd = jnp.dot(lcat, rcat, preferred_element_type=F32)
                inside = lax.broadcasted_iota(jnp.int32, (rest, nb), 1)
                inside = (inside >= r0) & (inside < r0 + block)
                m_re[f, r0 + block:, :] = jnp.where(inside, 0.0, m_re[f, r0 + block:, :]) - upd[:, :nb]
                m_im[f, r0 + block:, :] = jnp.where(inside, 0.0, m_im[f, r0 + block:, :]) - upd[:, nb:]
    for f in range(nf):
        w_re, w_im = w_ref[f, 0], w_ref[f, 1]
        rh, rl = split2(w_re)
        ih, il = split2(w_im)
        x_re, x_im = q_ref[f, 0], q_ref[f, 1]
        x = jnp.concatenate([x_re, x_im], axis=0)
        a = jnp.concatenate([rh, -ih], axis=1)
        al = jnp.concatenate([rl, -il], axis=1)
        b = jnp.concatenate([ih, rh], axis=1)
        bl = jnp.concatenate([il, rl], axis=1)
        out_ref[f, 0] = jnp.dot(a, x, preferred_element_type=F32) + jnp.dot(al, x, preferred_element_type=F32)
        out_ref[f, 1] = jnp.dot(b, x, preferred_element_type=F32) + jnp.dot(bl, x, preferred_element_type=F32)


def finish(q, g, scale, block=32):
    nf, _, nb, cells = q.shape
    vm = pl.BlockSpec(memory_space=pltpu.VMEM)
    return pl.pallas_call(
        functools.partial(factor_kernel, scale, block),
        out_shape=jax.ShapeDtypeStruct((nf, 2, nb, cells), F32),
        in_specs=[vm, vm], out_specs=vm,
        scratch_shapes=[pltpu.VMEM((nf, nb, nb), F32), pltpu.VMEM((nf, nb, nb), F32), pltpu.VMEM((nf, 2, nb, nb), F32)],
        compiler_params=pltpu.CompilerParams(vmem_limit_bytes=32 << 20),
        name="factor_apply",
    )(q, g)


def local(snapshots, frequencies, offsets):
    total_cells = snapshots.shape[2] * lax.axis_size("space")
    q, g = exchange(snapshots, frequencies, offsets)
    return finish(q, g, 1.0 / total_cells)


def solution(mesh):
    placed = (P("tm", None, "space"), P(), P("tm"))
    return jax.shard_map(
        local, mesh=mesh, in_specs=placed, out_specs=P("tm", None, None, "space"), check_vma=False
    )
```

time: 66.8 us -> 60.4 us (0.904)
  the two profiles are of different devices: /device:TPU:4 before, /device:TPU:1 now
where the time goes in v2:
time: 60.4 us; the launch traced here: 59.5 us
  Pallas kernels  57.7 us (96%)
  local copies, waits for them, and re-layouts  1.85 us (3%)
    pallas_call x1, Pallas kernels, exchange(): pl.pallas_call(functools.partial(exchange_kernel, nt, nx, nl, nh), out_sh...  39.3 us
    pallas_call x1, Pallas kernels, finish(): pl.pallas_call(functools.partial(factor_kernel, scale, block), out_shape=...  18.4 us
    unnamed x4, local copies, waits for them, and re-layouts  1.85 us

profile of v2, /device:TPU:1, one launch (start us, length us, event | category | flops | bytes accessed | tf_op | source)
XLA Modules:
  0.0 59.5 jit_solution(2294320768718226694)
XLA Ops:
  0.0 39.3 %exchange_gram.1 = (bf16[2,2,128,256]{3,2,1,0:T(8,128)(2,1)}, f32[256,128]{1,0:T(8,128)}) custom-call(s32[16]{0:T(128)} %freq_ref.1, s32[16]{0:T(128)} %off_ref.1, bf16[16,128,256]{2,1,0:T(8,128)(2,1)} %snap_hbm.1), custom_call_target="tpu_custom_call" | custom-call | tf_op jit(solution)/shard_map/exchange_gram/pallas_call | solution.py:217
  39.3 0.0 copy-start
  39.3 0.9 %copy-done = bf16[2,2,128,256]{3,2,1,0:T(8,128)(2,1)S(1)} copy-done((bf16[2,2,128,256]{3,2,1,0:T(8,128)(2,1)S(1)}, bf16[2,2,128,256]{3,2,1,0:T(8,128)(2,1)}, u32[]{:S(2)}) %copy-start) | copy-done | bytes 262168
  40.2 0.0 copy-start.1
  40.2 0.9 %copy-done.1 = f32[256,128]{1,0:T(8,128)S(1)} copy-done((f32[256,128]{1,0:T(8,128)S(1)}, f32[256,128]{1,0:T(8,128)}, u32[]{:S(2)}) %copy-start.1) | copy-done | bytes 131096
  41.1 18.4 %factor_apply.1 = f32[2,2,128,256]{3,2,1,0:T(8,128)} custom-call(bf16[2,2,128,256]{3,2,1,0:T(8,128)(2,1)S(1)} %copy-done, f32[2,128,128]{2,1,0:T(8,128)S(1)} %bitcast.1), custom_call_target="tpu_custom_call" | custom-call | tf_op jit(solution)/shard_map/factor_apply/pallas_call | solution.py:343
Async XLA Ops:
  39.3 1.0 %copy-start = (bf16[2,2,128,256]{3,2,1,0:T(8,128)(2,1)S(1)}, bf16[2,2,128,256]{3,2,1,0:T(8,128)(2,1)}, u32[]{:S(2)}) copy-start(bf16[2,2,128,256]{3,2,1,0:T(8,128)(2,1)} %get-tuple-element.7.q_ref) | copy-start | bytes 786436
  40.2 0.9 %copy-start.1 = (f32[256,128]{1,0:T(8,128)S(1)}, f32[256,128]{1,0:T(8,128)}, u32[]{:S(2)}) copy-start(f32[256,128]{1,0:T(8,128)} %get-tuple-element.8) | copy-start | bytes 393220

commit v3 on v2

--- a/solution.py
+++ b/solution.py
@@ -230,7 +230,7 @@
             dma((nh,)), dma((nh,)), dma((group,)), dma((group,)), dma((halves,)),
         ],
         compiler_params=pltpu.CompilerParams(
-            collective_id=0, has_side_effects=True, vmem_limit_bytes=63 << 20),
+            collective_id=0, has_side_effects=True, vmem_limit_bytes=53 << 20),
         name="exchange_gram",
     )(frequencies, offsets, snapshots)
     return q, g.reshape(nf, nb, nb)
@@ -244,6 +244,10 @@
 
 def lane_bcast(v, col):
     return jnp.broadcast_to(v[:, col:col + 1], v.shape)
+
+
+def row_bcast(v, s):
+    return jnp.broadcast_to(v[s:s + 1, :], v.shape)
 
 
 def factor_kernel(scale, block, q_ref, g_ref, out_ref, m_re, m_im, w_ref):
@@ -266,35 +270,42 @@
             for f in range(nf)
         ]
         dsel = [[jnp.ones((8, nb), F32) for v in range(per)] for f in range(nf)]
-        for p in range(block):
-            v0, s = p // 8, p % 8
-            col = r0 + p
-            at_col = lane8 == col
-            for f in range(nf):
-                re, im = R[f]
-                p_re = jnp.broadcast_to(re[v0][s:s + 1, :], (8, nb))
-                p_im = jnp.broadcast_to(im[v0][s:s + 1, :], (8, nb))
-                d = lane_bcast(p_re, col)
-                inv = 1.0 / d
-                dsel[f][v0] = jnp.where(row8 == s, d, dsel[f][v0])
-                u_re = jnp.where(at_col, inv, p_re * inv)
-                u_im = jnp.where(at_col, 0.0, p_im * inv)
-                for v in range(v0, per):
-                    if v == v0 and s == 7:
-                        continue
-                    c_re = lane_bcast(re[v], col)
-                    c_im = lane_bcast(im[v], col)
-                    if v == v0:
-                        below = row8 > s
-                        c_re = jnp.where(below, c_re, 0.0)
-                        c_im = jnp.where(below, c_im, 0.0)
-                        zap = at_col & below
-                    else:
-                        zap = at_col
-                    b_re = jnp.where(zap, 0.0, re[v])
-                    b_im = jnp.where(zap, 0.0, im[v])
-                    re[v] = b_re - (c_re * u_re - c_im * u_im)
-                    im[v] = b_im - (c_re * u_im + c_im * u_re)
+        for v0 in range(per):
+            c0 = r0 + 8 * v0
+            B = [
+                [[[lane_bcast(R[f][ri][v], c0 + c) for c in range(8)] for v in range(v0, per)] for ri in range(2)]
+                for f in range(nf)
+            ]
+            for s in range(8):
+                at_col = lane8 == c0 + s
+                below = row8 > s
+                for f in range(nf):
+                    re, im = R[f]
+                    b_re, b_im = B[f]
+                    d = row_bcast(b_re[0][s], s)
+                    ninv = -1.0 / d
+                    dsel[f][v0] = jnp.where(row8 == s, d, dsel[f][v0])
+                    p_re, p_im = row_bcast(re[v0], s), row_bcast(im[v0], s)
+                    h_re = [row_bcast(b_re[0][c], s) if c > s else None for c in range(8)]
+                    h_im = [row_bcast(b_im[0][c], s) if c > s else None for c in range(8)]
+                    for v in range(v0, per):
+                        i = v - v0
+                        if i == 0 and s == 7:
+                            continue
+                        n_re = b_re[i][s] * ninv
+                        n_im = b_im[i][s] * ninv
+                        if i == 0:
+                            n_re = jnp.where(below, n_re, 0.0)
+                            n_im = jnp.where(below, n_im, 0.0)
+                        for c in range(s + 1, 8):
+                            b_re[i][c], b_im[i][c] = (
+                                b_re[i][c] + (n_re * h_re[c] - n_im * h_im[c]),
+                                b_im[i][c] + (n_re * h_im[c] + n_im * h_re[c]),
+                            )
+                        re[v], im[v] = (
+                            jnp.where(at_col, n_re, re[v] + (n_re * p_re - n_im * p_im)),
+                            jnp.where(at_col, n_im, im[v] + (n_re * p_im + n_im * p_re)),
+                        )
         for f in range(nf):
             re, im = R[f]
             n_re, n_im = [], []
@@ -311,14 +322,14 @@
             w_ref[f, 1, r0:r0 + block, :] = jnp.where(keep, a_im, 0.0)
             if k + 1 < nb // block:
                 rest = nb - r0 - block
-                left = jnp.concatenate([a_re, a_im], axis=0).T[r0 + block:, :]
-                right = jnp.concatenate(
-                    [jnp.concatenate([a_re, a_im], axis=1), jnp.concatenate([a_im, -a_re], axis=1)], axis=0)
-                lh, ll = split2(left)
-                rh, rl = split2(right)
-                lcat = jnp.concatenate([lh, lh, ll], axis=1)
-                rcat = jnp.concatenate([rh, rl, rh], axis=0)
-                upd = jnp.dot(lcat, rcat, preferred_element_type=F32)
+                rh, rl = split2(a_re)
+                ih, il = split2(a_im)
+                lcat = jnp.concatenate([rh, ih, rh, ih, rl, il], axis=0)
+                rcat = jnp.concatenate(
+                    [jnp.concatenate([rh, ih, rl, il, rh, ih], axis=0),
+                     jnp.concatenate([ih, -rh, il, -rl, ih, -rh], axis=0)], axis=1)
+                upd = lax.dot_general(lcat, rcat, (((0,), (0,)), ((), ())), preferred_element_type=F32)
+                upd = upd[r0 + block:, :]
                 inside = lax.broadcasted_iota(jnp.int32, (rest, nb), 1)
                 inside = (inside >= r0) & (inside < r0 + block)
                 m_re[f, r0 + block:, :] = jnp.where(inside, 0.0, m_re[f, r0 + block:, :]) - upd[:, :nb]
@@ -337,7 +348,7 @@
         out_ref[f, 1] = jnp.dot(b, x, preferred_element_type=F32) + jnp.dot(bl, x, preferred_element_type=F32)
 
 
-def finish(q, g, scale, block=32):
+def finish(q, g, scale, block=16):
     nf, _, nb, cells = q.shape
     vm = pl.BlockSpec(memory_space=pltpu.VMEM)
     return pl.pallas_call(

time: 60.4 us -> 47.3 us (0.78)
  Pallas kernels: 57.7 us -> 45.1 us
    pallas_call x1, Pallas kernels: 18.4 us -> 6.75 us  [finish(): pl.pallas_call(functools.partial(factor_kernel, scale, block), out_shape=...]
    pallas_call x1, Pallas kernels: 39.3 us -> 38.4 us  [exchange(): pl.pallas_call(functools.partial(exchange_kernel, nt, nx, nl, nh), out_sh...]
where the time goes in v3:
time: 47.3 us; the launch traced here: 46.5 us
  Pallas kernels  45.1 us (95%)
  local copies, waits for them, and re-layouts  1.31 us (3%)
    pallas_call x1, Pallas kernels, exchange(): pl.pallas_call(functools.partial(exchange_kernel, nt, nx, nl, nh), out_sh...  38.4 us
    pallas_call x1, Pallas kernels, finish(): pl.pallas_call(functools.partial(factor_kernel, scale, block), out_shape=...  6.75 us
    unnamed x4, local copies, waits for them, and re-layouts  1.31 us

profile of v3, /device:TPU:1, one launch (start us, length us, event | category | flops | bytes accessed | tf_op | source)
XLA Modules:
  0.0 46.5 jit_solution(8508432791425161852)
XLA Ops:
  0.0 0.0 copy-start
  0.0 0.7 %copy-done = s32[16]{0:T(128)S(1)} copy-done((s32[16]{0:T(128)S(1)}, s32[16]{0:T(128)}, u32[]{:S(2)}) %copy-start) | copy-done | bytes 88
  0.7 0.0 copy-start.1
  0.7 0.7 %copy-done.1 = s32[16]{0:T(128)S(1)} copy-done((s32[16]{0:T(128)S(1)}, s32[16]{0:T(128)}, u32[]{:S(2)}) %copy-start.1) | copy-done | bytes 88
  1.3 38.4 %exchange_gram.1 = (bf16[2,2,128,256]{3,2,1,0:T(8,128)(2,1)S(1)}, f32[256,128]{1,0:T(8,128)S(1)}) custom-call(s32[16]{0:T(128)S(1)} %copy-done, s32[16]{0:T(128)S(1)} %copy-done.1, bf16[16,128,256]{2,1,0:T(8,128)(2,1)} %snap_hbm.1), custom_call_target="tpu_custom_call" | custom-call | tf_op jit(solution)/shard_map/exchange_gram/pallas_call | solution.py:217
  39.7 6.8 %factor_apply.1 = f32[2,2,128,256]{3,2,1,0:T(8,128)} custom-call(bf16[2,2,128,256]{3,2,1,0:T(8,128)(2,1)S(1)} %get-tuple-element.7.q_ref, f32[2,128,128]{2,1,0:T(8,128)S(1)} %bitcast.1), custom_call_target="tpu_custom_call" | custom-call | tf_op jit(solution)/shard_map/factor_apply/pallas_call | solution.py:354
Async XLA Ops:
  0.0 0.7 %copy-start = (s32[16]{0:T(128)S(1)}, s32[16]{0:T(128)}, u32[]{:S(2)}) copy-start(s32[16]{0:T(128)} %freq_ref.1) | copy-start | bytes 196
  0.7 0.7 %copy-start.1 = (s32[16]{0:T(128)S(1)}, s32[16]{0:T(128)}, u32[]{:S(2)}) copy-start(s32[16]{0:T(128)} %off_ref.1) | copy-start | bytes 196

commit v4 on v3

--- a/solution.py
+++ b/solution.py
@@ -33,8 +33,8 @@
 
 
 def exchange_kernel(
-    nt, nx, nl, nh, freq_ref, off_ref, snap_hbm, q_ref, g_ref,
-    snap, work, send, part, got, half_sum, got_far,
+    nt, nx, nl, nh, freq_hbm, off_hbm, snap_hbm, q_ref, g_ref,
+    freq_ref, off_ref, snap, work, send, part, got, half_sum, got_far,
     in_sem, a_send, a_recv, r_send, r_recv, f_send, f_recv, w_send, w_recv, own_sem,
 ):
     nf_all = freq_ref.shape[0]
@@ -62,16 +62,23 @@
     def far_peer(d):
         return (me, lax.rem(my_far + d, nh) * group + my_near)
 
-    near = [(dl, dx) for dl in range(nl) for dx in range(nx) if dl or dx]
+    order = (2, 1, 3, 0)
+    near = [(dl, dx) for dl in order for dx in order if dl or dx]
 
     barrier = pltpu.get_barrier_semaphore()
     for d in range(1, nh):
         pl.semaphore_signal(barrier, inc=1, device_id=far_peer(d), device_id_type=MESH)
+    for dl, dx in near:
+        pl.semaphore_signal(barrier, inc=1, device_id=near_peer(dl, dx), device_id_type=MESH)
     for d in range(1, nt):
         pl.semaphore_signal(barrier, inc=1, device_id=tm_peer(d), device_id_type=MESH)
-    for dl, dx in near:
-        pl.semaphore_signal(barrier, inc=1, device_id=near_peer(dl, dx), device_id_type=MESH)
-
+
+    small = [
+        pltpu.make_async_copy(freq_hbm, freq_ref, in_sem.at[4]),
+        pltpu.make_async_copy(off_hbm, off_ref, in_sem.at[5]),
+    ]
+    for load in small:
+        load.start()
     step = blocks // 4
     loads = [
         pltpu.make_async_copy(snap_hbm.at[pl.ds(i * step, step)], snap.at[pl.ds(i * step, step)], in_sem.at[i])
@@ -82,6 +89,8 @@
 
     row = lax.broadcasted_iota(jnp.int32, (nf_all, length), 0)
     position = lax.broadcasted_iota(jnp.int32, (nf_all, length), 1)
+    for load in small:
+        load.wait()
     freq = jnp.zeros((nf_all, length), jnp.int32)
     start = jnp.zeros((nf_all, length), jnp.int32)
     for j in range(nf_all):
@@ -108,97 +117,95 @@
 
     mine = pl.ds(pl.multiple_of(me * blocks, blocks), blocks)
 
-    def a_copy(h, d):
+    def a_copy(f, d):
         return pltpu.make_async_remote_copy(
-            src_ref=send.at[h, lax.rem(me + d, nt)],
-            dst_ref=q_ref.at[:, :, mine, pl.ds(h * LANES, LANES)],
-            send_sem=a_send.at[h, d], recv_sem=a_recv.at[h, d],
+            src_ref=send.at[f, lax.rem(me + d, nt)],
+            dst_ref=q_ref.at[f, :, mine, :],
+            send_sem=a_send.at[f, d], recv_sem=a_recv.at[f, d],
             device_id=tm_peer(d), device_id_type=MESH)
 
-    own = [
-        pltpu.make_async_copy(send.at[h, me], q_ref.at[:, :, mine, pl.ds(h * LANES, LANES)], own_sem.at[h])
-        for h in range(halves)
-    ]
-    for h in range(halves):
-        for j in range(nf_all):
+    own = [pltpu.make_async_copy(send.at[f, me], q_ref.at[f, :, mine, :], own_sem.at[f]) for f in range(nf)]
+    for f in range(nf):
+        for t in range(nt):
             for ri in range(2):
-                rows = work[h, pl.ds(ri * nf_all + j, blocks, stride=2 * nf_all), :]
-                send[h, j // nf, j % nf, ri] = rows.astype(BF16)
-        if h == 0:
+                for h in range(halves):
+                    rows = work[h, pl.ds(ri * nf_all + t * nf + f, blocks, stride=2 * nf_all), :]
+                    send[f, t, ri, :, h * LANES:(h + 1) * LANES] = rows.astype(BF16)
+        if f == 0:
             pl.semaphore_wait(barrier, nh - 1 + nt - 1 + group - 1)
         for d in range(1, nt):
-            a_copy(h, d).start()
-        own[h].start()
-    for h in range(halves):
-        own[h].wait()
-        for d in range(1, nt):
-            a_copy(h, d).wait_recv()
+            a_copy(f, d).start()
+        own[f].start()
 
     grow = lax.broadcasted_iota(jnp.int32, (nb, nb), 0)
     glane = lax.broadcasted_iota(jnp.int32, (nb, nb), 1)
-    for f in range(nf):
+    wide = nb // group
+
+    def chunk(slot):
+        return pl.ds(pl.multiple_of(slot * wide, wide), wide)
+
+    def r_copy(f, dl, dx):
+        i = dl * nx + dx
+        return pltpu.make_async_remote_copy(
+            src_ref=part.at[f, chunk(near_slot(dl, dx)), :], dst_ref=got.at[f, i],
+            send_sem=r_send.at[f, i], recv_sem=r_recv.at[f, i],
+            device_id=near_peer(dl, dx), device_id_type=MESH)
+
+    def f_copy(f, d):
+        return pltpu.make_async_remote_copy(
+            src_ref=half_sum.at[f], dst_ref=got_far.at[f, my_far],
+            send_sem=f_send.at[f, d], recv_sem=f_recv.at[f, d],
+            device_id=far_peer(d), device_id_type=MESH)
+
+    def w_copy(f, dl, dx):
+        i = dl * nx + dx
+        return pltpu.make_async_remote_copy(
+            src_ref=g_ref.at[f, chunk(my_near), :], dst_ref=g_ref.at[f, chunk(my_near), :],
+            send_sem=w_send.at[f, i], recv_sem=w_recv.at[f, i],
+            device_id=near_peer(dl, dx), device_id_type=MESH)
+
+    for f in range(nf):
+        own[f].wait()
+        for d in range(1, nt):
+            a_copy(f, d).wait_recv()
         rows = q_ref[f].reshape(2 * nb, cells)
         full = lax.dot_general(rows, rows, (((1,), (1,)), ((), ())), preferred_element_type=F32)
         real = full[:nb, :nb] + full[nb:, nb:]
         imag = full[nb:, :nb] - full[:nb, nb:]
-        part[f * nb:(f + 1) * nb, :] = jnp.where(grow >= glane, real, imag)
-
-    wide = nf * nb // group
-
-    def chunk(slot):
-        return pl.ds(pl.multiple_of(slot * wide, wide), wide)
-
-    def r_copy(dl, dx):
-        i = dl * nx + dx
-        return pltpu.make_async_remote_copy(
-            src_ref=part.at[chunk(near_slot(dl, dx)), :], dst_ref=got.at[i],
-            send_sem=r_send.at[i], recv_sem=r_recv.at[i],
-            device_id=near_peer(dl, dx), device_id_type=MESH)
-
-    for dl, dx in near:
-        r_copy(dl, dx).start()
-    total = part[chunk(my_near), :]
-    for dl, dx in near:
-        r_copy(dl, dx).wait_recv()
-        total = total + got[dl * nx + dx]
-    got_far[my_far] = total
-    half_sum[...] = total
-
-    def f_copy(d):
-        return pltpu.make_async_remote_copy(
-            src_ref=half_sum, dst_ref=got_far.at[my_far],
-            send_sem=f_send.at[d], recv_sem=f_recv.at[d],
-            device_id=far_peer(d), device_id_type=MESH)
-
-    for d in range(1, nh):
-        f_copy(d).start()
-    for d in range(1, nh):
-        f_copy(d).wait_recv()
-    total = got_far[0]
-    for i in range(1, nh):
-        total = total + got_far[i]
-    g_ref[chunk(my_near), :] = total
-
-    def w_copy(dl, dx):
-        i = dl * nx + dx
-        return pltpu.make_async_remote_copy(
-            src_ref=g_ref.at[chunk(my_near), :], dst_ref=g_ref.at[chunk(my_near), :],
-            send_sem=w_send.at[i], recv_sem=w_recv.at[i],
-            device_id=near_peer(dl, dx), device_id_type=MESH)
-
-    for dl, dx in near:
-        w_copy(dl, dx).start()
-    for h in range(halves):
+        part[f] = jnp.where(grow >= glane, real, imag)
+        for dl, dx in near:
+            r_copy(f, dl, dx).start()
+    for f in range(nf):
+        total = part[f, chunk(my_near), :]
+        for dl, dx in near:
+            r_copy(f, dl, dx).wait_recv()
+            total = total + got[f, dl * nx + dx]
+        got_far[f, my_far] = total
+        half_sum[f] = total
+        for d in (2, 1, 3):
+            f_copy(f, d).start()
+    for f in range(nf):
+        for d in range(1, nh):
+            f_copy(f, d).wait_recv()
+        total = got_far[f, 0]
+        for i in range(1, nh):
+            total = total + got_far[f, i]
+        g_ref[f, chunk(my_near), :] = total
+        for dl, dx in near:
+            w_copy(f, dl, dx).start()
+    for f in range(nf):
         for d in range(1, nt):
-            a_copy(h, d).wait_send()
-    for dl, dx in near:
-        r_copy(dl, dx).wait_send()
-    for d in range(1, nh):
-        f_copy(d).wait_send()
-    for dl, dx in near:
-        w_copy(dl, dx).wait_recv()
-    for dl, dx in near:
-        w_copy(dl, dx).wait_send()
+            a_copy(f, d).wait_send()
+        for dl, dx in near:
+            r_copy(f, dl, dx).wait_send()
+        for d in range(1, nh):
+            f_copy(f, d).wait_send()
+    for f in range(nf):
+        for dl, dx in near:
+            w_copy(f, dl, dx).wait_recv()
+    for f in range(nf):
+        for dl, dx in near:
+            w_copy(f, dl, dx).wait_send()
 
 
 def exchange(snapshots, frequencies, offsets):
@@ -209,31 +216,32 @@
     blocks, length, cells = snapshots.shape
     nf_all = frequencies.shape[0]
     nf, nb = nf_all // nt, blocks * nt
-    wide = nf * nb // group
+    wide = nb // group
     halves = cells // LANES
     vm = pl.BlockSpec(memory_space=pltpu.VMEM)
-    sm = pl.BlockSpec(memory_space=pltpu.SMEM)
     dma = pltpu.SemaphoreType.DMA
     q, g = pl.pallas_call(
         functools.partial(exchange_kernel, nt, nx, nl, nh),
-        out_shape=(jax.ShapeDtypeStruct((nf, 2, nb, cells), BF16), jax.ShapeDtypeStruct((nf * nb, nb), F32)),
-        in_specs=[sm, sm, pl.BlockSpec(memory_space=pltpu.HBM)], out_specs=(vm, vm),
+        out_shape=(jax.ShapeDtypeStruct((nf, 2, nb, cells), BF16), jax.ShapeDtypeStruct((nf, nb, nb), F32)),
+        in_specs=[pl.BlockSpec(memory_space=pltpu.HBM)] * 3, out_specs=(vm, vm),
         scratch_shapes=[
+            pltpu.SMEM((nf_all,), jnp.int32),
+            pltpu.SMEM((blocks,), jnp.int32),
             pltpu.VMEM((blocks, length, cells), BF16),
             pltpu.VMEM((halves, blocks * 2 * nf_all, LANES), F32),
-            pltpu.VMEM((halves, nt, nf, 2, blocks, LANES), BF16),
-            pltpu.VMEM((nf * nb, nb), F32),
-            pltpu.VMEM((group, wide, nb), F32),
-            pltpu.VMEM((wide, nb), F32),
-            pltpu.VMEM((nh, wide, nb), F32),
-            dma((4,)), dma((halves, nt)), dma((halves, nt)), dma((group,)), dma((group,)),
-            dma((nh,)), dma((nh,)), dma((group,)), dma((group,)), dma((halves,)),
+            pltpu.VMEM((nf, nt, 2, blocks, cells), BF16),
+            pltpu.VMEM((nf, nb, nb), F32),
+            pltpu.VMEM((nf, group, wide, nb), F32),
+            pltpu.VMEM((nf, wide, nb), F32),
+            pltpu.VMEM((nf, nh, wide, nb), F32),
+            dma((6,)), dma((nf, nt)), dma((nf, nt)), dma((nf, group)), dma((nf, group)),
+            dma((nf, nh)), dma((nf, nh)), dma((nf, group)), dma((nf, group)), dma((nf,)),
         ],
         compiler_params=pltpu.CompilerParams(
             collective_id=0, has_side_effects=True, vmem_limit_bytes=53 << 20),
         name="exchange_gram",
-    )(frequencies, offsets, snapshots)
-    return q, g.reshape(nf, nb, nb)
+    )(*[pltpu.with_memory_space_constraint(a, pltpu.HBM) for a in (frequencies, offsets, snapshots)])
+    return q, g
 
 
 def split2(v):

time: 47.3 us -> 45.2 us (0.956); the launches traced: 46.5 us -> 44.9 us
  local copies, waits for them, and re-layouts: 1.31 us -> 0 us
    unnamed x4 -> x0, local copies, waits for them, and re-layouts: 1.31 us -> none
where the time goes in v4:
time: 45.2 us; the launch traced here: 44.9 us
  Pallas kernels  44.9 us (99%)
    pallas_call x1, Pallas kernels, exchange(): pl.pallas_call(functools.partial(exchange_kernel, nt, nx, nl, nh), out_sh...  38.1 us
    pallas_call x1, Pallas kernels, finish(): pl.pallas_call(functools.partial(factor_kernel, scale, block), out_shape=...  6.75 us

profile of v4, /device:TPU:1, one launch (start us, length us, event | category | flops | bytes accessed | tf_op | source)
XLA Modules:
  0.0 44.9 jit_solution(4071006123001304113)
XLA Ops:
  0.0 38.1 %exchange_gram.1 = (bf16[2,2,128,256]{3,2,1,0:T(8,128)(2,1)S(1)}, f32[2,128,128]{2,1,0:T(8,128)S(1)}) custom-call(s32[16]{0:T(128)} %freq_hbm.1, s32[16]{0:T(128)} %off_hbm.1, bf16[16,128,256]{2,1,0:T(8,128)(2,1)} %snap_hbm.1), custom_call_target="tpu_custom_call" | custom-call | tf_op jit(solution)/shard_map/exchange_gram/pallas_call | solution.py:223
  38.1 6.7 %factor_apply.1 = f32[2,2,128,256]{3,2,1,0:T(8,128)} custom-call(bf16[2,2,128,256]{3,2,1,0:T(8,128)(2,1)S(1)} %get-tuple-element.7.q_ref, f32[2,128,128]{2,1,0:T(8,128)S(1)} %get-tuple-element.8.g_ref), custom_call_target="tpu_custom_call" | custom-call | tf_op jit(solution)/shard_map/factor_apply/pallas_call | solution.py:362

commit v5 on v4

--- a/solution.py
+++ b/solution.py
@@ -34,8 +34,8 @@
 
 def exchange_kernel(
     nt, nx, nl, nh, freq_hbm, off_hbm, snap_hbm, q_ref, g_ref,
-    freq_ref, off_ref, snap, work, send, part, got, half_sum, got_far,
-    in_sem, a_send, a_recv, r_send, r_recv, f_send, f_recv, w_send, w_recv, own_sem,
+    freq_ref, off_ref, snap, work, send, part, got, half_sum, got_far, final,
+    far_ok, in_sem, a_send, a_recv, r_send, r_recv, f_send, f_recv, w_send, w_recv, own_sem,
 ):
     nf_all = freq_ref.shape[0]
     blocks, length, cells = snap.shape
@@ -49,27 +49,59 @@
     my_near = lax.rem(spot, group)
     my_l = lax.div(my_near, nx)
     my_x = lax.rem(my_near, nx)
+    my_y = lax.div(me, 2)
+    core = lax.rem(me, 2)
+    owns = core * lax.div(lax.rem(my_l + 1, nl), 2)
+    flip = lax.div(my_far, 2)
+    my_m = (my_l - 1) + flip * (3 - 2 * my_l)
 
     def tm_peer(d):
         return (lax.rem(me + d, nt), spot)
 
-    def near_slot(dl, dx):
-        return lax.rem(my_l + dl, nl) * nx + lax.rem(my_x + dx, nx)
-
-    def near_peer(dl, dx):
-        return (me, my_far * group + near_slot(dl, dx))
-
-    def far_peer(d):
-        return (me, lax.rem(my_far + d, nh) * group + my_near)
+    def plane(far, m):
+        return 1 + m + lax.div(far, 2) * (1 - 2 * m)
+
+    def owner(m, dx):
+        return (2 * my_y + 1, my_far * group + plane(my_far, m) * nx + lax.rem(my_x + dx, nx))
+
+    def not_me(m, dx):
+        return (core == 0) | (my_l != plane(my_far, m)) if dx == 0 else my_x >= 0
+
+    def client(c, dl, dx):
+        return (2 * my_y + c, my_far * group + lax.rem(my_l + dl, nl) * nx + lax.rem(my_x + dx, nx))
+
+    def far_owner(d):
+        far = lax.rem(my_far + d, nh)
+        return (me, far * group + plane(far, my_m) * nx + my_x)
+
+    def rank(far):
+        return far + lax.div(far, 2) * (5 - 2 * far)
+
+    my_rank = rank(my_far)
+
+    def far_rank(d):
+        return rank(lax.rem(my_far + d, nh))
 
     order = (2, 1, 3, 0)
-    near = [(dl, dx) for dl in order for dx in order if dl or dx]
+    targets = [(m, dx) for dx in order for m in range(2)]
+    clients = [(c, dl, dx) for dx in order for dl in order for c in range(2) if dl or dx or c == 0]
 
     barrier = pltpu.get_barrier_semaphore()
-    for d in range(1, nh):
-        pl.semaphore_signal(barrier, inc=1, device_id=far_peer(d), device_id_type=MESH)
-    for dl, dx in near:
-        pl.semaphore_signal(barrier, inc=1, device_id=near_peer(dl, dx), device_id_type=MESH)
+
+    @pl.when(owns == 1)
+    def _():
+        for d in range(1, nh):
+            @pl.when(far_rank(d) > my_rank)
+            def _():
+                pl.semaphore_signal(barrier, inc=1, device_id=far_owner(d), device_id_type=MESH)
+        for c, dl, dx in clients:
+            pl.semaphore_signal(barrier, inc=1, device_id=client(c, dl, dx), device_id_type=MESH)
+
+    for m, dx in targets:
+        @pl.when(not_me(m, dx))
+        def _():
+            pl.semaphore_signal(barrier, inc=1, device_id=owner(m, dx), device_id_type=MESH)
+
     for d in range(1, nt):
         pl.semaphore_signal(barrier, inc=1, device_id=tm_peer(d), device_id_type=MESH)
 
@@ -132,37 +164,24 @@
                     rows = work[h, pl.ds(ri * nf_all + t * nf + f, blocks, stride=2 * nf_all), :]
                     send[f, t, ri, :, h * LANES:(h + 1) * LANES] = rows.astype(BF16)
         if f == 0:
-            pl.semaphore_wait(barrier, nh - 1 + nt - 1 + group - 1)
-        for d in range(1, nt):
+            pl.semaphore_wait(barrier, nt - 1 + 2 * nx + owns * (len(clients) - 1 + my_rank))
+        for d in (4, 3, 5, 2, 6, 1, 7):
             a_copy(f, d).start()
         own[f].start()
 
+    @pl.when(owns == 1)
+    def _():
+        for d in range(1, nh):
+            @pl.when(far_rank(d) < my_rank)
+            def _():
+                pl.semaphore_signal(far_ok.at[nh - d], inc=1, device_id=far_owner(d), device_id_type=MESH)
+
     grow = lax.broadcasted_iota(jnp.int32, (nb, nb), 0)
     glane = lax.broadcasted_iota(jnp.int32, (nb, nb), 1)
-    wide = nb // group
-
-    def chunk(slot):
-        return pl.ds(pl.multiple_of(slot * wide, wide), wide)
-
-    def r_copy(f, dl, dx):
-        i = dl * nx + dx
-        return pltpu.make_async_remote_copy(
-            src_ref=part.at[f, chunk(near_slot(dl, dx)), :], dst_ref=got.at[f, i],
-            send_sem=r_send.at[f, i], recv_sem=r_recv.at[f, i],
-            device_id=near_peer(dl, dx), device_id_type=MESH)
-
-    def f_copy(f, d):
-        return pltpu.make_async_remote_copy(
-            src_ref=half_sum.at[f], dst_ref=got_far.at[f, my_far],
-            send_sem=f_send.at[f, d], recv_sem=f_recv.at[f, d],
-            device_id=far_peer(d), device_id_type=MESH)
-
-    def w_copy(f, dl, dx):
-        i = dl * nx + dx
-        return pltpu.make_async_remote_copy(
-            src_ref=g_ref.at[f, chunk(my_near), :], dst_ref=g_ref.at[f, chunk(my_near), :],
-            send_sem=w_send.at[f, i], recv_sem=w_recv.at[f, i],
-            device_id=near_peer(dl, dx), device_id_type=MESH)
+    wide = nb // (2 * nx)
+
+    def chunk(m, x):
+        return pl.ds(pl.multiple_of((m * nx + x) * wide, wide), wide)
 
     for f in range(nf):
         own[f].wait()
@@ -173,39 +192,93 @@
         real = full[:nb, :nb] + full[nb:, nb:]
         imag = full[nb:, :nb] - full[:nb, nb:]
         part[f] = jnp.where(grow >= glane, real, imag)
-        for dl, dx in near:
-            r_copy(f, dl, dx).start()
-    for f in range(nf):
-        total = part[f, chunk(my_near), :]
-        for dl, dx in near:
-            r_copy(f, dl, dx).wait_recv()
-            total = total + got[f, dl * nx + dx]
-        got_far[f, my_far] = total
-        half_sum[f] = total
+
+    def r_copy(m, dx):
+        spot_there = lax.rem(my_l - plane(my_far, m) + nl, nl) * nx + (nx - dx) % nx
+        return pltpu.make_async_remote_copy(
+            src_ref=part.at[:, chunk(m, lax.rem(my_x + dx, nx)), :], dst_ref=got.at[core, spot_there],
+            send_sem=r_send.at[m, dx], recv_sem=r_recv.at[core, spot_there],
+            device_id=owner(m, dx), device_id_type=MESH)
+
+    for m, dx in targets:
+        @pl.when(not_me(m, dx))
+        def _():
+            r_copy(m, dx).start()
+
+    my_chunk = chunk(my_m, my_x)
+
+    def r_arrival(c, i):
+        return pltpu.make_async_remote_copy(
+            src_ref=half_sum.at[0], dst_ref=got.at[c, i], send_sem=r_send.at[0, 0], recv_sem=r_recv.at[c, i],
+            device_id=tm_peer(1), device_id_type=MESH)
+
+    def f_copy(d):
+        return pltpu.make_async_remote_copy(
+            src_ref=half_sum, dst_ref=got_far.at[my_far],
+            send_sem=f_send.at[d], recv_sem=f_recv.at[d],
+            device_id=far_owner(d), device_id_type=MESH)
+
+    def w_copy(c, dl, dx):
+        return pltpu.make_async_remote_copy(
+            src_ref=final.at[c], dst_ref=g_ref.at[:, my_chunk, :],
+            send_sem=w_send.at[c, dl * nx + dx], recv_sem=w_recv.at[my_m * nx + my_x],
+            device_id=client(c, dl, dx), device_id_type=MESH)
+
+    @pl.when(owns == 1)
+    def _():
+        for c in range(2):
+            total = part[:, my_chunk, :] if c == 1 else None
+            for i in range(group):
+                if c == 0 or i > 0:
+                    r_arrival(c, i).wait_recv()
+                    total = got[c, i] if total is None else total + got[c, i]
+            half_sum[c] = total
+            got_far[my_far, c] = total
         for d in (2, 1, 3):
-            f_copy(f, d).start()
-    for f in range(nf):
-        for d in range(1, nh):
-            f_copy(f, d).wait_recv()
-        total = got_far[f, 0]
-        for i in range(1, nh):
-            total = total + got_far[f, i]
-        g_ref[f, chunk(my_near), :] = total
-        for dl, dx in near:
-            w_copy(f, dl, dx).start()
+            @pl.when(far_rank(d) < my_rank)
+            def _():
+                f_copy(d).start()
+        for d in (1, 3, 2):
+            @pl.when(far_rank(d) > my_rank)
+            def _():
+                pl.semaphore_wait(far_ok.at[d], 1)
+                f_copy(d).start()
+        for d in (1, 3, 2):
+            f_copy(d).wait_recv()
+        for c in range(2):
+            total = got_far[0, c]
+            for i in range(1, nh):
+                total = total + got_far[i, c]
+            final[c] = total
+        for c, dl, dx in clients:
+            w_copy(c, dl, dx).start()
+        g_ref[:, my_chunk, :] = final[1]
+
+    def w_arrival(slot):
+        return pltpu.make_async_remote_copy(
+            src_ref=final.at[0], dst_ref=g_ref.at[:, pl.ds(slot * wide, wide), :],
+            send_sem=w_send.at[0, 0], recv_sem=w_recv.at[slot],
+            device_id=tm_peer(1), device_id_type=MESH)
+
+    for slot in range(2 * nx):
+        @pl.when((owns == 0) | (my_m * nx + my_x != slot))
+        def _():
+            w_arrival(slot).wait_recv()
+
     for f in range(nf):
         for d in range(1, nt):
             a_copy(f, d).wait_send()
-        for dl, dx in near:
-            r_copy(f, dl, dx).wait_send()
+    for m, dx in targets:
+        @pl.when(not_me(m, dx))
+        def _():
+            r_copy(m, dx).wait_send()
+
+    @pl.when(owns == 1)
+    def _():
         for d in range(1, nh):
-            f_copy(f, d).wait_send()
-    for f in range(nf):
-        for dl, dx in near:
-            w_copy(f, dl, dx).wait_recv()
-    for f in range(nf):
-        for dl, dx in near:
-            w_copy(f, dl, dx).wait_send()
+            f_copy(d).wait_send()
+        for c, dl, dx in clients:
+            w_copy(c, dl, dx).wait_send()
 
 
 def exchange(snapshots, frequencies, offsets):
@@ -216,7 +289,7 @@
     blocks, length, cells = snapshots.shape
     nf_all = frequencies.shape[0]
     nf, nb = nf_all // nt, blocks * nt
-    wide = nb // group
+    wide = nb // (2 * nx)
     halves = cells // LANES
     vm = pl.BlockSpec(memory_space=pltpu.VMEM)
     dma = pltpu.SemaphoreType.DMA
@@ -231,11 +304,12 @@
             pltpu.VMEM((halves, blocks * 2 * nf_all, LANES), F32),
             pltpu.VMEM((nf, nt, 2, blocks, cells), BF16),
             pltpu.VMEM((nf, nb, nb), F32),
-            pltpu.VMEM((nf, group, wide, nb), F32),
-            pltpu.VMEM((nf, wide, nb), F32),
-            pltpu.VMEM((nf, nh, wide, nb), F32),
-            dma((6,)), dma((nf, nt)), dma((nf, nt)), dma((nf, group)), dma((nf, group)),
-            dma((nf, nh)), dma((nf, nh)), dma((nf, group)), dma((nf, group)), dma((nf,)),
+            pltpu.VMEM((2, group, nf, wide, nb), F32),
+            pltpu.VMEM((2, nf, wide, nb), F32),
+            pltpu.VMEM((nh, 2, nf, wide, nb), F32),
+            pltpu.VMEM((2, nf, wide, nb), F32),
+            pltpu.SemaphoreType.REGULAR((nh,)), dma((6,)), dma((nf, nt)), dma((nf, nt)), dma((2, nx)), dma((2, group)),
+            dma((nh,)), dma((nh,)), dma((2, group)), dma((2 * nx,)), dma((nf,)),
         ],
         compiler_params=pltpu.CompilerParams(
             collective_id=0, has_side_effects=True, vmem_limit_bytes=53 << 20),

time: 45.2 us -> 44.6 us (0.987)
  no operation moved by 1% of the time
where the time goes in v5:
time: 44.6 us; the launch traced here: 44.5 us
  Pallas kernels  44.5 us (100%)
    pallas_call x1, Pallas kernels, exchange(): pl.pallas_call(functools.partial(exchange_kernel, nt, nx, nl, nh), out_sh...  37.8 us
    pallas_call x1, Pallas kernels, finish(): pl.pallas_call(functools.partial(factor_kernel, scale, block), out_shape=...  6.75 us

profile of v5, /device:TPU:1, one launch (start us, length us, event | category | flops | bytes accessed | tf_op | source)
XLA Modules:
  0.0 44.5 jit_solution(5356970122659391369)
XLA Ops:
  0.0 37.8 %exchange_gram.1 = (bf16[2,2,128,256]{3,2,1,0:T(8,128)(2,1)S(1)}, f32[2,128,128]{2,1,0:T(8,128)S(1)}) custom-call(s32[16]{0:T(128)} %freq_hbm.1, s32[16]{0:T(128)} %off_hbm.1, bf16[16,128,256]{2,1,0:T(8,128)(2,1)} %snap_hbm.1), custom_call_target="tpu_custom_call" | custom-call | tf_op jit(solution)/shard_map/exchange_gram/pallas_call | solution.py:296
  37.8 6.7 %factor_apply.1 = f32[2,2,128,256]{3,2,1,0:T(8,128)} custom-call(bf16[2,2,128,256]{3,2,1,0:T(8,128)(2,1)S(1)} %get-tuple-element.7.q_ref, f32[2,128,128]{2,1,0:T(8,128)S(1)} %get-tuple-element.8.g_ref), custom_call_target="tpu_custom_call" | custom-call | tf_op jit(solution)/shard_map/factor_apply/pallas_call | solution.py:436

commit v6 on v5

--- a/solution.py
+++ b/solution.py
@@ -84,7 +84,7 @@
 
     order = (2, 1, 3, 0)
     targets = [(m, dx) for dx in order for m in range(2)]
-    clients = [(c, dl, dx) for dx in order for dl in order for c in range(2) if dl or dx or c == 0]
+    clients = [(c, dl, dx) for c in (1, 0) for dx in order for dl in order if dl or dx or c == 0]
 
     barrier = pltpu.get_barrier_semaphore()
 

time: 44.6 us -> 44 us (0.987)
  Pallas kernels: 44.5 us -> 43.8 us
    pallas_call x1, Pallas kernels: 37.8 us -> 37.1 us  [exchange(): pl.pallas_call(functools.partial(exchange_kernel, nt, nx, nl, nh), out_sh...]
where the time goes in v6:
time: 44 us; the launch traced here: 43.9 us
  Pallas kernels  43.8 us (100%)
    pallas_call x1, Pallas kernels, exchange(): pl.pallas_call(functools.partial(exchange_kernel, nt, nx, nl, nh), out_sh...  37.1 us
    pallas_call x1, Pallas kernels, finish(): pl.pallas_call(functools.partial(factor_kernel, scale, block), out_shape=...  6.75 us

profile of v6, /device:TPU:1, one launch (start us, length us, event | category | flops | bytes accessed | tf_op | source)
XLA Modules:
  0.0 43.9 jit_solution(17655121282663658940)
XLA Ops:
  0.0 37.1 %exchange_gram.1 = (bf16[2,2,128,256]{3,2,1,0:T(8,128)(2,1)S(1)}, f32[2,128,128]{2,1,0:T(8,128)S(1)}) custom-call(s32[16]{0:T(128)} %freq_hbm.1, s32[16]{0:T(128)} %off_hbm.1, bf16[16,128,256]{2,1,0:T(8,128)(2,1)} %snap_hbm.1), custom_call_target="tpu_custom_call" | custom-call | tf_op jit(solution)/shard_map/exchange_gram/pallas_call | solution.py:296
  37.1 6.7 %factor_apply.1 = f32[2,2,128,256]{3,2,1,0:T(8,128)} custom-call(bf16[2,2,128,256]{3,2,1,0:T(8,128)(2,1)S(1)} %get-tuple-element.7.q_ref, f32[2,128,128]{2,1,0:T(8,128)S(1)} %get-tuple-element.8.g_ref), custom_call_target="tpu_custom_call" | custom-call | tf_op jit(solution)/shard_map/factor_apply/pallas_call | solution.py:436

commit v7 on v6

--- a/solution.py
+++ b/solution.py
@@ -212,10 +212,10 @@
             src_ref=half_sum.at[0], dst_ref=got.at[c, i], send_sem=r_send.at[0, 0], recv_sem=r_recv.at[c, i],
             device_id=tm_peer(1), device_id_type=MESH)
 
-    def f_copy(d):
-        return pltpu.make_async_remote_copy(
-            src_ref=half_sum, dst_ref=got_far.at[my_far],
-            send_sem=f_send.at[d], recv_sem=f_recv.at[d],
+    def f_copy(c, d):
+        return pltpu.make_async_remote_copy(
+            src_ref=half_sum.at[c], dst_ref=got_far.at[my_far, c],
+            send_sem=f_send.at[c, d], recv_sem=f_recv.at[c, d],
             device_id=far_owner(d), device_id_type=MESH)
 
     def w_copy(c, dl, dx):
@@ -226,7 +226,7 @@
 
     @pl.when(owns == 1)
     def _():
-        for c in range(2):
+        for c in (1, 0):
             total = part[:, my_chunk, :] if c == 1 else None
             for i in range(group):
                 if c == 0 or i > 0:
@@ -234,24 +234,26 @@
                     total = got[c, i] if total is None else total + got[c, i]
             half_sum[c] = total
             got_far[my_far, c] = total
-        for d in (2, 1, 3):
-            @pl.when(far_rank(d) < my_rank)
-            def _():
-                f_copy(d).start()
-        for d in (1, 3, 2):
-            @pl.when(far_rank(d) > my_rank)
-            def _():
-                pl.semaphore_wait(far_ok.at[d], 1)
-                f_copy(d).start()
-        for d in (1, 3, 2):
-            f_copy(d).wait_recv()
-        for c in range(2):
+            for d in (2, 1, 3):
+                @pl.when(far_rank(d) < my_rank)
+                def _():
+                    f_copy(c, d).start()
+            for d in (1, 3, 2):
+                @pl.when(far_rank(d) > my_rank)
+                def _():
+                    if c == 1:
+                        pl.semaphore_wait(far_ok.at[d], 1)
+                    f_copy(c, d).start()
+        for c in (1, 0):
+            for d in (1, 3, 2):
+                f_copy(c, d).wait_recv()
             total = got_far[0, c]
             for i in range(1, nh):
                 total = total + got_far[i, c]
             final[c] = total
-        for c, dl, dx in clients:
-            w_copy(c, dl, dx).start()
+            for cc, dl, dx in clients:
+                if cc == c:
+                    w_copy(cc, dl, dx).start()
         g_ref[:, my_chunk, :] = final[1]
 
     def w_arrival(slot):
@@ -275,8 +277,9 @@
 
     @pl.when(owns == 1)
     def _():
-        for d in range(1, nh):
-            f_copy(d).wait_send()
+        for c in range(2):
+            for d in range(1, nh):
+                f_copy(c, d).wait_send()
         for c, dl, dx in clients:
             w_copy(c, dl, dx).wait_send()
 
@@ -309,7 +312,7 @@
             pltpu.VMEM((nh, 2, nf, wide, nb), F32),
             pltpu.VMEM((2, nf, wide, nb), F32),
             pltpu.SemaphoreType.REGULAR((nh,)), dma((6,)), dma((nf, nt)), dma((nf, nt)), dma((2, nx)), dma((2, group)),
-            dma((nh,)), dma((nh,)), dma((2, group)), dma((2 * nx,)), dma((nf,)),
+            dma((2, nh)), dma((2, nh)), dma((2, group)), dma((2 * nx,)), dma((nf,)),
         ],
         compiler_params=pltpu.CompilerParams(
             collective_id=0, has_side_effects=True, vmem_limit_bytes=53 << 20),

time: 44 us -> 43.2 us (0.982)
  Pallas kernels: 43.8 us -> 43.1 us
    pallas_call x1, Pallas kernels: 37.1 us -> 36.4 us  [exchange(): pl.pallas_call(functools.partial(exchange_kernel, nt, nx, nl, nh), out_sh...]
where the time goes in v7:
time: 43.2 us; the launch traced here: 43.1 us
  Pallas kernels  43.1 us (100%)
    pallas_call x1, Pallas kernels, exchange(): pl.pallas_call(functools.partial(exchange_kernel, nt, nx, nl, nh), out_sh...  36.4 us
    pallas_call x1, Pallas kernels, finish(): pl.pallas_call(functools.partial(factor_kernel, scale, block), out_shape=...  6.75 us

profile of v7, /device:TPU:1, one launch (start us, length us, event | category | flops | bytes accessed | tf_op | source)
XLA Modules:
  0.0 43.1 jit_solution(15530323163703995794)
XLA Ops:
  0.0 36.4 %exchange_gram.1 = (bf16[2,2,128,256]{3,2,1,0:T(8,128)(2,1)S(1)}, f32[2,128,128]{2,1,0:T(8,128)S(1)}) custom-call(s32[16]{0:T(128)} %freq_hbm.1, s32[16]{0:T(128)} %off_hbm.1, bf16[16,128,256]{2,1,0:T(8,128)(2,1)} %snap_hbm.1), custom_call_target="tpu_custom_call" | custom-call | tf_op jit(solution)/shard_map/exchange_gram/pallas_call | solution.py:299
  36.4 6.7 %factor_apply.1 = f32[2,2,128,256]{3,2,1,0:T(8,128)} custom-call(bf16[2,2,128,256]{3,2,1,0:T(8,128)(2,1)S(1)} %get-tuple-element.7.q_ref, f32[2,128,128]{2,1,0:T(8,128)S(1)} %get-tuple-element.8.g_ref), custom_call_target="tpu_custom_call" | custom-call | tf_op jit(solution)/shard_map/factor_apply/pallas_call | solution.py:439
